TPU v7x, 256 devices: a whole 4x4x8 slice. The times are simulated.
256 devices in a mesh: dp: 16 (over z_lo, x), seq: 16 (over z_hi, y, core).
Axes of the slice: x: 4, y: 4, z: 8 (z_hi: 2, z_lo: 4; z = z_hi * 4 + z_lo), core: 2. Of those that a mesh axis runs over, the one named last changes fastest.
Arguments:
- frames: bfloat16 [16, 4096, 1280], P('dp', 'seq'), may hold values from -6 to 6
- live: int32 [16, 4096], P('dp', 'seq'), may hold values from 0 to 1
- norm_gain: float32 [1280], replicated, may hold values from 0.25 to 1.75
- w_qkv: bfloat16 [1280, 1920], P('dp')
- w_out: bfloat16 [640, 1280], P('dp'), may hold values from -0.25 to 0.25
- cotangent: bfloat16 [16, 4096, 1280], P('dp', 'seq'), may hold values from -6 to 6
Outputs:
- grad_frames: bfloat16 [16, 4096, 1280], P('dp', 'seq')
- grad_qkv: float32 [1280, 1920], P('dp', 'seq')
- grad_out: float32 [640, 1280], P('dp', 'seq')
All inputs are finite; a program needn't handle non-finite values.
Results may differ from a plain program's by a relative error of at most 0.0095.
Values may be sent and summed in bfloat16 or wider, within the bound.
No kernel may reach another device: no remote copies, remote signals or barrier semaphores. Data moves between devices by JAX's collectives and lax.ppermute only.
A program may use at most 64 MiB of HBM per device.

v0:
```python
import math
import jax
import jax.numpy as jnp
from jax import lax
from jax.sharding import PartitionSpec as P

HEAD_DIM = 64
WIN = 512
EPS = 1e-05
NEG = -1e30


def from_behind(value, axis, steps):
    count = lax.axis_size(axis)
    leading, last = (max(0, -steps), min(count, count - steps))
    return lax.ppermute(value, axis, [(source, source + steps) for source in range(leading, last)])


def norm_rows(values_in):
    average = jnp.mean(values_in, axis=-1, keepdims=True)
    centred = values_in - average
    inverse = lax.rsqrt(jnp.mean(centred * centred, axis=-1, keepdims=True) + EPS)
    return (centred * inverse, inverse)


def against(left, right):
    return lax.dot_general(
        left, right, (((1,), (1,)), ((), ())), preferred_element_type=jnp.float32
    )


def leading(left, right):
    return lax.dot_general(
        left, right, (((0,), (0,)), ((), ())), preferred_element_type=jnp.float32
    )


def head_terms(query_head, key_head, value_head, grad_head, allowed, query_live, score_scale):
    scores = jnp.where(allowed, against(query_head, key_head) * score_scale, NEG)
    row_peak = jnp.max(scores, axis=-1, keepdims=True)
    exponent = jnp.exp(scores - row_peak)
    probabilities = exponent / jnp.sum(exponent, axis=-1, keepdims=True)
    probs_b = probabilities.astype(jnp.bfloat16)
    mixed = jnp.dot(probs_b, value_head, preferred_element_type=jnp.float32) * query_live[:, None]
    attended = mixed.astype(jnp.bfloat16)
    row_delta = jnp.sum(grad_head.astype(jnp.float32) * attended.astype(jnp.float32), axis=1)
    grad_probs = against(grad_head, value_head)
    grad_scores = (probabilities * (grad_probs - row_delta[:, None]) * score_scale).astype(
        jnp.bfloat16
    )
    grad_query = jnp.dot(grad_scores, key_head, preferred_element_type=jnp.float32)
    grad_key = leading(grad_scores, query_head)
    grad_value = leading(probs_b, grad_head)
    return (attended, grad_query, grad_key, grad_value)


def body(frames, live, norm_gain, w_qkv, w_out, cotangent):
    length = frames.shape[1]
    n_data = lax.axis_size("dp")
    n_seq = lax.axis_size("seq")
    full_qkv, full_out = (
        lax.all_gather(w_qkv, "dp", axis=0, tiled=True),
        lax.all_gather(w_out, "dp", axis=0, tiled=True),
    )
    inner = full_out.shape[0]
    heads = inner // HEAD_DIM
    hidden = frames[0].astype(jnp.float32)
    unit_rows, inverse = norm_rows(hidden)
    normed = (unit_rows * norm_gain).astype(jnp.bfloat16)
    projected = jnp.dot(normed, full_qkv, preferred_element_type=jnp.float32).astype(jnp.bfloat16)
    query = projected[:, :inner]
    key_values = projected[:, inner:]
    live_row = live[0]
    query_live = live_row.astype(jnp.float32)
    live_mark = live_row.astype(jnp.bfloat16)
    upstream = cotangent[0]
    grad_att = (against(upstream, full_out) * query_live[:, None]).astype(jnp.bfloat16)
    neighbours = -(-WIN // length)
    offsets = list(range(neighbours, 0, -1)) + list(range(-1, -neighbours - 1, -1))
    before_pairs, before_marks, after_pairs, after_marks = ([], [], [], [])
    for offset in offsets:
        distance = abs(offset)
        row_count = min(length, WIN - (distance - 1) * length)
        if offset > 0:
            send_pairs = key_values
            send_marks = live_mark
        else:
            send_pairs = key_values
            send_marks = live_mark
        got_pairs, got_marks = from_behind((send_pairs, send_marks), "seq", offset)
        if offset > 0:
            before_pairs.append(got_pairs)
            before_marks.append(got_marks)
        else:
            after_pairs.append(got_pairs)
            after_marks.append(got_marks)
    ext_pairs = jnp.concatenate(before_pairs + [key_values] + after_pairs, axis=0)
    ext_live = jnp.concatenate(before_marks + [live_mark] + after_marks, axis=0).astype(jnp.float32)
    total_span = length + 2 * WIN
    block_rows = min(length, 512)
    key_span = block_rows + 2 * WIN
    query_pos = jnp.arange(block_rows, dtype=jnp.int32)
    key_pos = jnp.arange(key_span, dtype=jnp.int32) - WIN
    in_window = jnp.abs(query_pos[:, None] - key_pos[None, :]) <= WIN
    allowances = [in_window & (ext_live[None, :] > 0.5)]
    score_scale = 1.0 / math.sqrt(HEAD_DIM)

    def split_heads(matrix):
        return matrix.reshape(matrix.shape[0], heads, HEAD_DIM).transpose(1, 0, 2)

    def merge_heads(matrix):
        return matrix.transpose(1, 0, 2).reshape(matrix.shape[1], inner)

    def one_head(inputs):
        query_head, key_head, value_head, grad_head = inputs
        out_blocks, query_blocks = ([], [])
        key_grads = jnp.zeros((total_span, HEAD_DIM), jnp.float32)
        value_grads = jnp.zeros((total_span, HEAD_DIM), jnp.float32)
        attended, grad_query, grad_key, grad_value = head_terms(
            query_head, key_head, value_head, grad_head, allowances[0], query_live, score_scale
        )
        out_blocks.append(attended)
        query_blocks.append(grad_query)
        key_grads = key_grads.at[0:key_span].add(grad_key)
        value_grads = value_grads.at[0:key_span].add(grad_value)
        return (
            jnp.concatenate(out_blocks, axis=0),
            jnp.concatenate(query_blocks, axis=0),
            key_grads,
            value_grads,
        )

    att_heads, query_heads, key_heads, value_heads = lax.map(
        one_head,
        (
            split_heads(query),
            split_heads(ext_pairs[:, :inner]),
            split_heads(ext_pairs[:, inner:]),
            split_heads(grad_att),
        ),
    )
    attention = merge_heads(att_heads)
    grad_query = merge_heads(query_heads)
    ext_grads = jnp.concatenate([merge_heads(key_heads), merge_heads(value_heads)], axis=1)
    own_grads = ext_grads[WIN : WIN + length]
    for offset in offsets:
        distance = abs(offset)
        row_count = min(length, WIN - (distance - 1) * length)
        if offset > 0:
            first_row = WIN - distance * length + length - row_count
        else:
            first_row = WIN + length + (distance - 1) * length
        arrived = from_behind(ext_grads[first_row : first_row + row_count], "seq", -offset)
        if offset > 0:
            own_grads = own_grads.at[length - row_count :].add(arrived)
        else:
            own_grads = own_grads.at[:row_count].add(arrived)
    grad_projected = jnp.concatenate([grad_query, own_grads], axis=1).astype(jnp.bfloat16)
    grad_unit = against(grad_projected, full_qkv) * norm_gain
    through = inverse * (
        grad_unit
        - jnp.mean(grad_unit, axis=-1, keepdims=True)
        - unit_rows * jnp.mean(grad_unit * unit_rows, axis=-1, keepdims=True)
    )
    grad_rows = (upstream.astype(jnp.float32) + through).astype(jnp.bfloat16)[None]
    factor = 1.0 / math.sqrt(n_data * n_seq * length)
    term_qkv = leading(normed, grad_projected)
    term_out = leading(attention, upstream)
    part_qkv, part_out = (
        lax.psum_scatter(term_qkv, "seq", scatter_dimension=1, tiled=True),
        lax.psum_scatter(term_out, "seq", scatter_dimension=1, tiled=True),
    )
    sum_qkv, sum_out = (
        lax.psum_scatter(part_qkv, "dp", scatter_dimension=0, tiled=True),
        lax.psum_scatter(part_out, "dp", scatter_dimension=0, tiled=True),
    )
    return (grad_rows, sum_qkv * factor, sum_out * factor)


def solution(mesh):
    return jax.shard_map(
        body,
        mesh=mesh,
        in_specs=(
            P("dp", "seq", None),
            P("dp", "seq"),
            P(),
            P("dp", None),
            P("dp", None),
            P("dp", "seq", None),
        ),
        out_specs=(P("dp", "seq", None), P("dp", "seq"), P("dp", "seq")),
        check_vma=False,
    )
```

profile of v0, /device:TPU:8, one launch (start us, length us, event | category | flops | bytes accessed | tf_op | source)
XLA Modules:
  0.0 898.2 jit_solution(4358646345607529689)
XLA Ops:
  9.4 3.5 collective-permute-start.4
  14.8 3.6 collective-permute-start.6
  22.0 79.7 %all-gather.3.cloned.1.call-done = bf16[1280,1920]{1,0:T(8,128)(2,1)} async-done(((bf16[80,1920]{1,0:T(8,128)(2,1)}), bf16[1280,1920]{1,0:T(8,128)(2,1)}) %all-gather.3.cloned.1.call-update) | async-done | bytes 4915216 | tf_op jit(solution)/shard_map/all_gather | solution.py:62
  101.7 4.0 convolution_convert_fusion
  107.6 3.3 collective-permute-start
  113.9 70.7 %all-gather.5.cloned.1.call-done = bf16[640,1280]{1,0:T(8,128)(2,1)} async-done(((bf16[40,1280]{1,0:T(8,128)(2,1)}), bf16[640,1280]{1,0:T(8,128)(2,1)}) %all-gather.5.cloned.1.call-update) | async-done | bytes 1638416 | tf_op jit(solution)/shard_map/all_gather | solution.py:63
  184.5 3.1 fusion.61
  199.4 5.4 collective-permute-done.2
  206.0 9.9 %collective-permute-done.3 = bf16[256,1280]{1,0:T(8,128)(2,1)} collective-permute-done((bf16[256,1280]{1,0:T(8,128)(2,1)}, bf16[256,1280]{1,0:T(8,128)(2,1)}, u32[]{:S(2)}, u32[]{:S(2)}) %collective-permute-start.3) | collective-permute-done | bytes 655392 | tf_op jit(solution)/shard_map/ppermute | solution.py:16
  217.0 2.0 fusion.73
  219.0 3.6 copy.25
  222.6 3.5 copy.26
  226.1 109.6 %while.32 = (s32[]{:T(128)}, bf16[10,256,64]{1,2,0:T(8,128)(2,1)}, bf16[10,256,64]{1,2,0:T(8,128)(2,1)}, f32[10,1280,64]{1,2,0:T(8,128)S(1)}, f32[10,1280,64]{1,...) while((s32[]{:T(128)}, bf16[10,256,64]{1,2,0:T(8,128)(2,1)}, ...), condition=%wide.region_6.7_spmd.clone, body=%wide.region_2.6_spmd.clone.sunk | while | flops 258637056 | bytes 10183041 | solution.py:133
  241.0 2.0 bitcast_dynamic-update-slice_fusion.2
  262.9 2.0 bitcast_dynamic-update-slice_fusion.2
  284.8 2.0 bitcast_dynamic-update-slice_fusion.2
  306.7 2.0 bitcast_dynamic-update-slice_fusion.2
  335.7 3.6 fusion.63
  339.4 2.2 fusion.59
  343.6 8.6 collective-permute-start.11
  354.2 3.1 collective-permute-start.9
  357.3 14.8 %collective-permute-done.10 = f32[256,1280]{0,1:T(8,128)S(1)} collective-permute-done((f32[256,1280]{0,1:T(8,128)S(1)}, f32[256,1280]{0,1:T(8,128)S(1)}, u32[]{:S(2)}, u32[]{:S(2)}) %collective-permute-start.10) | collective-permute-done | bytes 1310752 | tf_op jit(solution)/shard_map/ppermute | solution.py:16
  372.1 9.2 %collective-permute-done.11 = f32[256,1280]{0,1:T(8,128)S(1)} collective-permute-done((f32[256,1280]{0,1:T(8,128)S(1)}, f32[256,1280]{0,1:T(8,128)S(1)}, u32[]{:S(2)}, u32[]{:S(2)}) %collective-permute-start.11) | collective-permute-done | bytes 1310752 | tf_op jit(solution)/shard_map/ppermute | solution.py:16
  381.4 4.1 collective-permute-done.8
  385.5 14.1 %collective-permute-done.9 = f32[256,1280]{0,1:T(8,128)S(1)} collective-permute-done((f32[256,1280]{0,1:T(8,128)S(1)}, f32[256,1280]{0,1:T(8,128)S(1)}, u32[]{:S(2)}, u32[]{:S(2)}) %collective-permute-start.9) | collective-permute-done | bytes 1310752 | tf_op jit(solution)/shard_map/ppermute | solution.py:16
  400.8 5.3 fusion.66
  406.3 88.3 %reduce-scatter.9.cloned.1.call-done = f32[640,80]{0,1:T(8,128)} async-done(((f32[640,1280]{0,1:T(8,128)}), f32[640,80]{0,1:T(8,128)}) %reduce-scatter.9.cloned.1.call-update) | async-done | bytes 204816 | tf_op jit(solution)/shard_map/reduce_scatter | solution.py:171
  495.8 153.3 %reduce-scatter.7.cloned.1.call-done = f32[1280,120]{0,1:T(8,128)} async-done(((f32[1280,1920]{0,1:T(8,128)}), f32[1280,120]{0,1:T(8,128)}) %reduce-scatter.7.cloned.1.call-update) | async-done | bytes 614416 | tf_op jit(solution)/shard_map/reduce_scatter | solution.py:170
  649.2 2.2 copy.33
  651.4 4.2 fusion.71
  657.0 146.1 %all-reduce.3.cloned.1.call-done = f32[640,80]{0,1:T(8,128)} async-done(((f32[640,80]{0,1:T(8,128)}), f32[640,80]{0,1:T(8,128)}) %all-reduce.3.cloned.1.call-update) | async-done | bytes 204816
  804.8 85.0 %reduce-scatter.11.cloned.1.call-done = f32[80,120]{1,0:T(8,128)} async-done(((f32[1280,120]{1,0:T(8,128)}), f32[80,120]{1,0:T(8,128)}) %reduce-scatter.11.cloned.1.call-update) | async-done | bytes 38416
  (165 shorter events, 138.5 us)
Async XLA Ops:
  7.2 14.5 %copy-start.1 = (bf16[1,256,1280]{2,1,0:T(8,128)(2,1)S(1)}, bf16[1,256,1280]{2,1,0:T(8,128)(2,1)}, u32[]{:S(2)}) copy-start(bf16[1,256,1280]{2,1,0:T(8,128)(2,1)} %param.32) | copy-start | bytes 1966084
  7.2 94.5 %copy-start.11 = (f32[1280]{0:T(1024)S(1)}, f32[1280]{0:T(1024)}, u32[]{:S(2)}) copy-start(f32[1280]{0:T(1024)} %param.34) | copy-start | bytes 15364
  7.2 94.5 %all-gather.3.cloned.1.call-start = ((), (), s32[]{:S(2)}) async-start(), calls=%async_computation.3 | async-start | bytes 5222400 | tf_op jit(solution)/shard_map/all_gather | solution.py:62
  7.9 176.6 %all-gather.5.cloned.1.call-start = ((), (), s32[]{:S(2)}) async-start(), calls=%async_computation.4 | async-start | bytes 1740800 | tf_op jit(solution)/shard_map/all_gather | solution.py:63
  8.7 485.8 %reduce-scatter.9.cloned.1.call-start = ((), (), s32[]{:S(2)}) async-start(), calls=%async_computation.6 | async-start | bytes 3481600 | tf_op jit(solution)/shard_map/reduce_scatter | solution.py:171
  9.4 101.6 %collective-permute-start.4 = (bf16[256]{0:T(256)(128)(2,1)S(1)}, bf16[256]{0:T(256)(128)(2,1)S(1)}, u32[]{:S(2)}, u32[]{:S(2)}) collective-permute-start(bf16[256]{0:T(256)(128)(2,1)S(1)} %convert_reduce_fusion.1), channel_id=1, source_target_pairs={{0,2},{1,3},{2,4},{3,5},{4,6},{5,7},{6,8},{7,9},{8,10},{9,11},{10,... | collective-permute-start | bytes 1544 | tf_op jit(solution)/shard_map/ppermute | solution.py:16
  12.9 98.4 %collective-permute-start.5 = (bf16[256]{0:T(256)(128)(2,1)S(1)}, bf16[256]{0:T(256)(128)(2,1)S(1)}, u32[]{:S(2)}, u32[]{:S(2)}) collective-permute-start(bf16[256]{0:T(256)(128)(2,1)S(1)} %convert_reduce_fusion.1), channel_id=1, source_target_pairs={{0,1},{1,2},{2,3},{3,4},{4,5},{5,6},{6,7},{7,8},{8,9},{9,10},{10,1... | collective-permute-start | bytes 1544 | tf_op jit(solution)/shard_map/ppermute | solution.py:16
  14.8 96.9 %collective-permute-start.6 = (bf16[256]{0:T(256)(128)(2,1)S(1)}, bf16[256]{0:T(256)(128)(2,1)S(1)}, u32[]{:S(2)}, u32[]{:S(2)}) collective-permute-start(bf16[256]{0:T(256)(128)(2,1)S(1)} %convert_reduce_fusion.1), channel_id=1, source_target_pairs={{1,0},{2,1},{3,2},{4,3},{5,4},{6,5},{7,6},{8,7},{9,8},{10,9},{11,1... | collective-permute-start | bytes 1544 | tf_op jit(solution)/shard_map/ppermute | solution.py:16
  18.5 93.4 %collective-permute-start.7 = (bf16[256]{0:T(256)(128)(2,1)S(1)}, bf16[256]{0:T(256)(128)(2,1)S(1)}, u32[]{:S(2)}, u32[]{:S(2)}) collective-permute-start(bf16[256]{0:T(256)(128)(2,1)S(1)} %convert_reduce_fusion.1), channel_id=1, source_target_pairs={{2,0},{3,1},{4,2},{5,3},{6,4},{7,5},{8,6},{9,7},{10,8},{11,9},{12,... | collective-permute-start | bytes 1544 | tf_op jit(solution)/shard_map/ppermute | solution.py:16
  105.7 1.0 copy-start.4
  106.7 4.2 copy-start.12
  107.6 89.4 %collective-permute-start = (bf16[256,1280]{1,0:T(8,128)(2,1)}, bf16[256,1280]{1,0:T(8,128)(2,1)}, u32[]{:S(2)}, u32[]{:S(2)}) collective-permute-start(bf16[256,1280]{1,0:T(8,128)(2,1)} %slice.121), channel_id=1, source_target_pairs={{0,2},{1,3},{2,4},{3,5},{4,6},{5,7},{6,8},{7,9},{8,10},{9,11},{10,... | collective-permute-start | bytes 1966088 | tf_op jit(solution)/shard_map/ppermute | solution.py:16
  111.9 86.3 %collective-permute-start.1 = (bf16[256,1280]{1,0:T(8,128)(2,1)}, bf16[256,1280]{1,0:T(8,128)(2,1)}, u32[]{:S(2)}, u32[]{:S(2)}) collective-permute-start(bf16[256,1280]{1,0:T(8,128)(2,1)} %slice.121), channel_id=1, source_target_pairs={{0,1},{1,2},{2,3},{3,4},{4,5},{5,6},{6,7},{7,8},{8,9},{9,10},{10,1... | collective-permute-start | bytes 1966088 | tf_op jit(solution)/shard_map/ppermute | solution.py:16
  189.5 15.3 %collective-permute-start.2 = (bf16[256,1280]{1,0:T(8,128)(2,1)}, bf16[256,1280]{1,0:T(8,128)(2,1)}, u32[]{:S(2)}, u32[]{:S(2)}) collective-permute-start(bf16[256,1280]{1,0:T(8,128)(2,1)} %slice.121), channel_id=1, source_target_pairs={{1,0},{2,1},{3,2},{4,3},{5,4},{6,5},{7,6},{8,7},{9,8},{10,9},{11,1... | collective-permute-start | bytes 1966088 | tf_op jit(solution)/shard_map/ppermute | solution.py:16
  191.4 24.4 %collective-permute-start.3 = (bf16[256,1280]{1,0:T(8,128)(2,1)}, bf16[256,1280]{1,0:T(8,128)(2,1)}, u32[]{:S(2)}, u32[]{:S(2)}) collective-permute-start(bf16[256,1280]{1,0:T(8,128)(2,1)} %slice.121), channel_id=1, source_target_pairs={{2,0},{3,1},{4,2},{5,3},{6,4},{7,5},{8,6},{9,7},{10,8},{11,9},{12,... | collective-permute-start | bytes 1966088 | tf_op jit(solution)/shard_map/ppermute | solution.py:16
  197.0 2.4 copy-start.5
  339.4 309.8 %reduce-scatter.7.cloned.1.call-start = ((), (), s32[]{:S(2)}) async-start(), calls=%async_computation.5 | async-start | bytes 10444800 | tf_op jit(solution)/shard_map/reduce_scatter | solution.py:170
  339.4 60.1 %copy-start = (f32[10,1280,64]{1,2,0:T(8,128)S(1)}, f32[10,1280,64]{1,2,0:T(8,128)}, u32[]{:S(2)}) copy-start(f32[10,1280,64]{1,2,0:T(8,128)} %get-tuple-element.301) | copy-start | bytes 9830404
  341.6 30.5 %collective-permute-start.10 = (f32[256,1280]{0,1:T(8,128)S(1)}, f32[256,1280]{0,1:T(8,128)S(1)}, u32[]{:S(2)}, u32[]{:S(2)}) collective-permute-start(f32[256,1280]{0,1:T(8,128)S(1)} %get-tuple-element.397), channel_id=1, source_target_pairs={{0,1},{1,2},{2,3},{3,4},{4,5},{5,6},{6,7},{7,8},{8,9},{9,10},{10,1... | collective-permute-start | bytes 3932168 | tf_op jit(solution)/shard_map/ppermute | solution.py:16
  343.6 37.8 %collective-permute-start.11 = (f32[256,1280]{0,1:T(8,128)S(1)}, f32[256,1280]{0,1:T(8,128)S(1)}, u32[]{:S(2)}, u32[]{:S(2)}) collective-permute-start(f32[256,1280]{0,1:T(8,128)S(1)} %get-tuple-element.396), channel_id=1, source_target_pairs={{0,2},{1,3},{2,4},{3,5},{4,6},{5,7},{6,8},{7,9},{8,10},{9,11},{10,... | collective-permute-start | bytes 3932168 | tf_op jit(solution)/shard_map/ppermute | solution.py:16
  352.2 33.3 %collective-permute-start.8 = (f32[256,1280]{0,1:T(8,128)S(1)}, f32[256,1280]{0,1:T(8,128)S(1)}, u32[]{:S(2)}, u32[]{:S(2)}) collective-permute-start(f32[256,1280]{0,1:T(8,128)S(1)} %get-tuple-element.394), channel_id=1, source_target_pairs={{2,0},{3,1},{4,2},{5,3},{6,4},{7,5},{8,6},{9,7},{10,8},{11,9},{12,... | collective-permute-start | bytes 3932168 | tf_op jit(solution)/shard_map/ppermute | solution.py:16
  354.1 46.7 %copy-start.2 = (bf16[1,256,1280]{2,1,0:T(8,128)(2,1)S(1)}, bf16[1,256,1280]{2,1,0:T(8,128)(2,1)}, u32[]{:S(2)}) copy-start(bf16[1,256,1280]{2,1,0:T(8,128)(2,1)} %param.32) | copy-start | bytes 1966084
  354.1 46.7 %copy-start.9 = (bf16[10,256,64]{1,2,0:T(8,128)(2,1)S(1)}, bf16[10,256,64]{1,2,0:T(8,128)(2,1)}, u32[]{:S(2)}) copy-start(bf16[10,256,64]{1,2,0:T(8,128)(2,1)} %get-tuple-element.299) | copy-start | bytes 983044
  354.2 45.4 %collective-permute-start.9 = (f32[256,1280]{0,1:T(8,128)S(1)}, f32[256,1280]{0,1:T(8,128)S(1)}, u32[]{:S(2)}, u32[]{:S(2)}) collective-permute-start(f32[256,1280]{0,1:T(8,128)S(1)} %get-tuple-element.395), channel_id=1, source_target_pairs={{1,0},{2,1},{3,2},{4,3},{5,4},{6,5},{7,6},{8,7},{9,8},{10,9},{11,1... | collective-permute-start | bytes 3932168 | tf_op jit(solution)/shard_map/ppermute | solution.py:16
  400.0 0.8 copy-start.6
  406.1 88.4 %copy-start.13 = (u32[256]{0:T(256)S(1)}, u32[256]{0:T(256)}, u32[]{:S(2)}) copy-start(u32[256]{0:T(256)} %constant.302) | copy-start | bytes 3076
  406.2 245.2 %copy-start.3 = (bf16[1,256,1280]{2,1,0:T(8,128)(2,1)S(1)}, bf16[1,256,1280]{2,1,0:T(8,128)(2,1)}, u32[]{:S(2)}) copy-start(bf16[1,256,1280]{2,1,0:T(8,128)(2,1)} %param.32) | copy-start | bytes 1966084
  406.2 245.2 %copy-start.7 = (bf16[256,1280]{0,1:T(8,128)(2,1)S(1)}, bf16[256,1280]{0,1:T(8,128)(2,1)}, u32[]{:S(2)}) copy-start(bf16[256,1280]{0,1:T(8,128)(2,1)} %copy-done.6) | copy-start | bytes 1966084
  406.2 245.2 %copy-start.10 = (bf16[10,256,64]{1,2,0:T(8,128)(2,1)S(1)}, bf16[10,256,64]{1,2,0:T(8,128)(2,1)}, u32[]{:S(2)}) copy-start(bf16[10,256,64]{1,2,0:T(8,128)(2,1)} %get-tuple-element.299) | copy-start | bytes 983044
  406.2 396.9 %all-reduce.3.cloned.1.call-start = ((), (), s32[]{:S(2)}) async-start(), calls=%async_computation.8 | async-start | bytes 409600
  494.5 395.2 %reduce-scatter.11.cloned.1.call-start = ((), (), s32[]{:S(2)}) async-start(), calls=%async_computation.7 | async-start | bytes 696320
  651.4 4.3 copy-start.8
Sparse Core Ops, SparseCore 0:
  9.8 91.8 all-gather.2
  103.5 81.0 all-gather.4
  339.5 155.0 reduce-scatter.8
  499.1 149.9 reduce-scatter.6
  651.6 151.4 all-reduce.2
  805.5 84.2 reduce-scatter.10
where the time goes:
time: 902 us; the launch traced here: 898 us
  waiting for transfers between devices  682 us (76%)
  matrix products  118 us (13%)
  starting transfers between devices  35.9 us (4%)
  local copies, waits for them, and re-layouts  27.9 us (3%)
  other arithmetic  18.6 us (2%)
  between operations  15.2 us (2%)
    unnamed x8, waiting for transfers between devices  233 us
    reduce_scatter x1, waiting for transfers between devices, body(): lax.psum_scatter(term_qkv, 'seq', scatter_dimension=1, tiled=True)  153 us
    reduce_scatter x1, waiting for transfers between devices, body(): lax.psum_scatter(term_out, 'seq', scatter_dimension=1, tiled=True)  88.3 us
    all_gather x1, waiting for transfers between devices, body(): lax.all_gather(w_qkv, 'dp', axis=0, tiled=True)  79.7 us
    all_gather x1, waiting for transfers between devices, body(): lax.all_gather(w_out, 'dp', axis=0, tiled=True)  70.7 us
    ppermute x12, waiting for transfers between devices, from_behind(): lax.ppermute(value, axis, [(source, source + steps) for source in range(l...  57.6 us
    dot_general x22, matrix products, against(): lax.dot_general(left, right, (((1,), (1,)), ((), ())), preferred_element_...  38 us
    dot_general x22, matrix products, leading(): lax.dot_general(left, right, (((0,), (0,)), ((), ())), preferred_element_...  38 us
  transfers between devices with their start and end apart: 18, of which 12 were waited for; matrix products, arithmetic and copies ran while one was open for 4% of the time, Pallas kernels for 0%

commit v1 on v0

--- a/solution.py
+++ b/solution.py
@@ -59,7 +59,9 @@
     n_data = lax.axis_size("dp")
     n_seq = lax.axis_size("seq")
     full_qkv, full_out = (
-        lax.all_gather(w_qkv, "dp", axis=0, tiled=True),
+        jnp.concatenate(
+            lax.all_to_all(jnp.stack([w_qkv] * lax.axis_size("dp")), "dp", 0, 0), axis=0
+        ),
         lax.all_gather(w_out, "dp", axis=0, tiled=True),
     )
     inner = full_out.shape[0]

time: 902 us -> 894 us (level)
  waiting for transfers between devices: 682 us -> 665 us
    all_to_all x0 -> x1, waiting for transfers between devices: none -> 96.4 us  [body(): lax.all_to_all(jnp.stack([w_qkv] * lax.axis_size('dp')), 'dp', 0, 0)]
    all_gather x1 -> x0, waiting for transfers between devices: 79.7 us -> none  [body(): lax.all_gather(w_qkv, 'dp', axis=0, tiled=True)]
    all_gather x1, waiting for transfers between devices: 70.7 us -> 0.02 us  [body(): lax.all_gather(w_out, 'dp', axis=0, tiled=True)]
    reduce_scatter x1, waiting for transfers between devices: 88.3 us -> 128 us  [body(): lax.psum_scatter(term_out, 'seq', scatter_dimension=1, tiled=True)]
    unnamed x8 -> x7, waiting for transfers between devices: 233 us -> 232 us
where the time goes in v1:
time: 894 us; the launch traced here: 890 us
  waiting for transfers between devices  665 us (74%)
  matrix products  119 us (13%)
  starting transfers between devices  43.7 us (5%)
  local copies, waits for them, and re-layouts  31.4 us (4%)
  other arithmetic  16.9 us (2%)
  between operations  14.8 us (2%)
    unnamed x7, waiting for transfers between devices  232 us
    reduce_scatter x1, waiting for transfers between devices, body(): lax.psum_scatter(term_qkv, 'seq', scatter_dimension=1, tiled=True)  154 us
    reduce_scatter x1, waiting for transfers between devices, body(): lax.psum_scatter(term_out, 'seq', scatter_dimension=1, tiled=True)  128 us
    all_to_all x1, waiting for transfers between devices, body(): lax.all_to_all(jnp.stack([w_qkv] * lax.axis_size('dp')), 'dp', 0, 0)  96.4 us
    ppermute x12, waiting for transfers between devices, from_behind(): lax.ppermute(value, axis, [(source, source + steps) for source in range(l...  55.2 us
    dot_general x22, matrix products, against(): lax.dot_general(left, right, (((1,), (1,)), ((), ())), preferred_element_...  38 us
    dot_general x22, matrix products, leading(): lax.dot_general(left, right, (((0,), (0,)), ((), ())), preferred_element_...  38 us
    ppermute x12, starting transfers between devices, from_behind(): lax.ppermute(value, axis, [(source, source + steps) for source in range(l...  34.9 us
  transfers between devices with their start and end apart: 18, of which 12 were waited for; matrix products, arithmetic and copies ran while one was open for 4% of the time, Pallas kernels for 0%

profile of v1, /device:TPU:8, one launch (start us, length us, event | category | flops | bytes accessed | tf_op | source)
XLA Modules:
  0.0 890.3 jit_solution(14534896186449436055)
XLA Ops:
  7.2 3.5 stack.2
  10.7 8.6 all-to-all-start
  20.1 3.5 collective-permute-start.4
  25.6 3.6 collective-permute-start.6
  31.7 96.4 %all-to-all-done = bf16[16,80,1920]{2,1,0:T(8,128)(2,1)} async-done(((bf16[16,80,1920]{2,1,0:T(8,128)(2,1)}), bf16[16,80,1920]{2,1,0:T(8,128)(2,1)}, u32[]{:S(2)}, u32[]{:S(2)}) %all-to-all-start) | async-done | bytes 4915232 | tf_op jit(solution)/shard_map/all_to_all | solution.py:63
  128.0 4.0 convolution_convert_fusion
  133.9 3.5 collective-permute-start
  140.4 3.1 fusion.64
  145.4 3.6 collective-permute-start.2
  155.8 2.0 collective-permute-done.1
  158.9 4.1 collective-permute-done.2
  164.2 9.0 %collective-permute-done.3 = bf16[256,1280]{1,0:T(8,128)(2,1)} collective-permute-done((bf16[256,1280]{1,0:T(8,128)(2,1)}, bf16[256,1280]{1,0:T(8,128)(2,1)}, u32[]{:S(2)}, u32[]{:S(2)}) %collective-permute-start.3) | collective-permute-done | bytes 655392 | tf_op jit(solution)/shard_map/ppermute | solution.py:16
  174.3 2.0 fusion.83
  176.3 3.6 copy.25
  179.9 3.5 copy.26
  183.4 109.8 %while.32 = (s32[]{:T(128)}, bf16[10,256,64]{1,2,0:T(8,128)(2,1)}, bf16[10,256,64]{1,2,0:T(8,128)(2,1)}, f32[10,1280,64]{1,2,0:T(8,128)S(1)}, f32[10,1280,64]{1,...) while((s32[]{:T(128)}, bf16[10,256,64]{1,2,0:T(8,128)(2,1)}, ...), condition=%wide.region_6.7_spmd.clone, body=%wide.region_2.6_spmd.clone.sunk | while | flops 258637056 | bytes 10183041 | solution.py:135
  209.3 2.0 bitcast_dynamic-update-slice_fusion.2
  293.2 3.6 fusion.70
  296.9 2.2 fusion.62
  301.0 6.0 collective-permute-start.11
  309.0 3.1 collective-permute-start.9
  312.1 17.4 %collective-permute-done.10 = f32[256,1280]{0,1:T(8,128)S(1)} collective-permute-done((f32[256,1280]{0,1:T(8,128)S(1)}, f32[256,1280]{0,1:T(8,128)S(1)}, u32[]{:S(2)}, u32[]{:S(2)}) %collective-permute-start.10) | collective-permute-done | bytes 1310752 | tf_op jit(solution)/shard_map/ppermute | solution.py:16
  329.6 6.6 collective-permute-done.11
  336.2 9.0 %collective-permute-done.8 = f32[256,1280]{0,1:T(8,128)S(1)} collective-permute-done((f32[256,1280]{0,1:T(8,128)S(1)}, f32[256,1280]{0,1:T(8,128)S(1)}, u32[]{:S(2)}, u32[]{:S(2)}) %collective-permute-start.8) | collective-permute-done | bytes 1310752 | tf_op jit(solution)/shard_map/ppermute | solution.py:16
  345.2 7.0 collective-permute-done.9
  353.5 5.3 fusion.67
  358.9 127.6 %reduce-scatter.9.cloned.1.call-done = f32[640,80]{0,1:T(8,128)} async-done(((f32[640,1280]{0,1:T(8,128)}), f32[640,80]{0,1:T(8,128)}) %reduce-scatter.9.cloned.1.call-update) | async-done | bytes 204816 | tf_op jit(solution)/shard_map/reduce_scatter | solution.py:173
  487.8 153.5 %reduce-scatter.7.cloned.1.call-done = f32[1280,120]{0,1:T(8,128)} async-done(((f32[1280,1920]{0,1:T(8,128)}), f32[1280,120]{0,1:T(8,128)}) %reduce-scatter.7.cloned.1.call-update) | async-done | bytes 614416 | tf_op jit(solution)/shard_map/reduce_scatter | solution.py:172
  641.4 2.2 copy.33
  643.6 4.2 fusion.81
  649.2 146.3 %all-reduce.3.cloned.1.call-done = f32[640,80]{0,1:T(8,128)} async-done(((f32[640,80]{0,1:T(8,128)}), f32[640,80]{0,1:T(8,128)}) %all-reduce.3.cloned.1.call-update) | async-done | bytes 204816
  797.2 85.0 %reduce-scatter.11.cloned.1.call-done = f32[80,120]{1,0:T(8,128)} async-done(((f32[1280,120]{1,0:T(8,128)}), f32[80,120]{1,0:T(8,128)}) %reduce-scatter.11.cloned.1.call-update) | async-done | bytes 38416
  (165 shorter events, 140.1 us)
Async XLA Ops:
  10.7 9.5 %copy-start.12 = (s32[1,256]{1,0:T(1,128)S(1)}, s32[1,256]{1,0:T(1,128)}, u32[]{:S(2)}) copy-start(s32[1,256]{1,0:T(1,128)} %param.33) | copy-start | bytes 3076
  10.7 20.5 %copy-start.1 = (bf16[1,256,1280]{2,1,0:T(8,128)(2,1)S(1)}, bf16[1,256,1280]{2,1,0:T(8,128)(2,1)}, u32[]{:S(2)}) copy-start(bf16[1,256,1280]{2,1,0:T(8,128)(2,1)} %param.32) | copy-start | bytes 1966084
  10.7 117.3 %all-to-all-start = ((bf16[16,80,1920]{2,1,0:T(8,128)(2,1)}), bf16[16,80,1920]{2,1,0:T(8,128)(2,1)}, u32[]{:S(2)}, u32[]{:S(2)}) async-start(bf16[16,80,1920]{2,1,0:T(8,128)(2,1)} %stack.2), calls=%async_computation | async-start | bytes 9830400 | tf_op jit(solution)/shard_map/all_to_all | solution.py:63
  19.3 108.7 %copy-start.11 = (f32[1280]{0:T(1024)S(1)}, f32[1280]{0:T(1024)}, u32[]{:S(2)}) copy-start(f32[1280]{0:T(1024)} %param.34) | copy-start | bytes 15364
  19.3 121.0 %all-gather.2.cloned.1.call-start = ((), (), s32[]{:S(2)}) async-start(), calls=%async_computation.4 | async-start | bytes 1740800 | tf_op jit(solution)/shard_map/all_gather | solution.py:65
  20.1 466.4 %reduce-scatter.9.cloned.1.call-start = ((), (), s32[]{:S(2)}) async-start(), calls=%async_computation.6 | async-start | bytes 3481600 | tf_op jit(solution)/shard_map/reduce_scatter | solution.py:173
  20.1 117.3 %collective-permute-start.4 = (bf16[256]{0:T(256)(128)(2,1)S(1)}, bf16[256]{0:T(256)(128)(2,1)S(1)}, u32[]{:S(2)}, u32[]{:S(2)}) collective-permute-start(bf16[256]{0:T(256)(128)(2,1)S(1)} %convert_reduce_fusion.1), channel_id=1, source_target_pairs={{0,2},{1,3},{2,4},{3,5},{4,6},{5,7},{6,8},{7,9},{8,10},{9,11},{10,... | collective-permute-start | bytes 1544 | tf_op jit(solution)/shard_map/ppermute | solution.py:16
  23.6 114.1 %collective-permute-start.5 = (bf16[256]{0:T(256)(128)(2,1)S(1)}, bf16[256]{0:T(256)(128)(2,1)S(1)}, u32[]{:S(2)}, u32[]{:S(2)}) collective-permute-start(bf16[256]{0:T(256)(128)(2,1)S(1)} %convert_reduce_fusion.1), channel_id=1, source_target_pairs={{0,1},{1,2},{2,3},{3,4},{4,5},{5,6},{6,7},{7,8},{8,9},{9,10},{10,1... | collective-permute-start | bytes 1544 | tf_op jit(solution)/shard_map/ppermute | solution.py:16
  25.6 112.6 %collective-permute-start.6 = (bf16[256]{0:T(256)(128)(2,1)S(1)}, bf16[256]{0:T(256)(128)(2,1)S(1)}, u32[]{:S(2)}, u32[]{:S(2)}) collective-permute-start(bf16[256]{0:T(256)(128)(2,1)S(1)} %convert_reduce_fusion.1), channel_id=1, source_target_pairs={{1,0},{2,1},{3,2},{4,3},{5,4},{6,5},{7,6},{8,7},{9,8},{10,9},{11,1... | collective-permute-start | bytes 1544 | tf_op jit(solution)/shard_map/ppermute | solution.py:16
  29.2 109.2 %collective-permute-start.7 = (bf16[256]{0:T(256)(128)(2,1)S(1)}, bf16[256]{0:T(256)(128)(2,1)S(1)}, u32[]{:S(2)}, u32[]{:S(2)}) collective-permute-start(bf16[256]{0:T(256)(128)(2,1)S(1)} %convert_reduce_fusion.1), channel_id=1, source_target_pairs={{2,0},{3,1},{4,2},{5,3},{6,4},{7,5},{8,6},{9,7},{10,8},{11,9},{12,... | collective-permute-start | bytes 1544 | tf_op jit(solution)/shard_map/ppermute | solution.py:16
  132.1 1.0 copy-start.4
  133.9 20.6 %collective-permute-start = (bf16[256,1280]{1,0:T(8,128)(2,1)}, bf16[256,1280]{1,0:T(8,128)(2,1)}, u32[]{:S(2)}, u32[]{:S(2)}) collective-permute-start(bf16[256,1280]{1,0:T(8,128)(2,1)} %slice.121), channel_id=1, source_target_pairs={{0,2},{1,3},{2,4},{3,5},{4,6},{5,7},{6,8},{7,9},{8,10},{9,11},{10,... | collective-permute-start | bytes 1966088 | tf_op jit(solution)/shard_map/ppermute | solution.py:16
  138.4 19.4 %collective-permute-start.1 = (bf16[256,1280]{1,0:T(8,128)(2,1)}, bf16[256,1280]{1,0:T(8,128)(2,1)}, u32[]{:S(2)}, u32[]{:S(2)}) collective-permute-start(bf16[256,1280]{1,0:T(8,128)(2,1)} %slice.121), channel_id=1, source_target_pairs={{0,1},{1,2},{2,3},{3,4},{4,5},{5,6},{6,7},{7,8},{8,9},{9,10},{10,1... | collective-permute-start | bytes 1966088 | tf_op jit(solution)/shard_map/ppermute | solution.py:16
  145.4 17.7 %collective-permute-start.2 = (bf16[256,1280]{1,0:T(8,128)(2,1)}, bf16[256,1280]{1,0:T(8,128)(2,1)}, u32[]{:S(2)}, u32[]{:S(2)}) collective-permute-start(bf16[256,1280]{1,0:T(8,128)(2,1)} %slice.121), channel_id=1, source_target_pairs={{1,0},{2,1},{3,2},{4,3},{5,4},{6,5},{7,6},{8,7},{9,8},{10,9},{11,1... | collective-permute-start | bytes 1966088 | tf_op jit(solution)/shard_map/ppermute | solution.py:16
  149.0 24.2 %collective-permute-start.3 = (bf16[256,1280]{1,0:T(8,128)(2,1)}, bf16[256,1280]{1,0:T(8,128)(2,1)}, u32[]{:S(2)}, u32[]{:S(2)}) collective-permute-start(bf16[256,1280]{1,0:T(8,128)(2,1)} %slice.121), channel_id=1, source_target_pairs={{2,0},{3,1},{4,2},{5,3},{6,4},{7,5},{8,6},{9,7},{10,8},{11,9},{12,... | collective-permute-start | bytes 1966088 | tf_op jit(solution)/shard_map/ppermute | solution.py:16
  154.5 4.4 copy-start.5
  296.8 344.5 %reduce-scatter.7.cloned.1.call-start = ((), (), s32[]{:S(2)}) async-start(), calls=%async_computation.5 | async-start | bytes 10444800 | tf_op jit(solution)/shard_map/reduce_scatter | solution.py:172
  296.9 55.3 %copy-start = (f32[10,1280,64]{1,2,0:T(8,128)S(1)}, f32[10,1280,64]{1,2,0:T(8,128)}, u32[]{:S(2)}) copy-start(f32[10,1280,64]{1,2,0:T(8,128)} %get-tuple-element.301) | copy-start | bytes 9830404
  299.1 30.5 %collective-permute-start.10 = (f32[256,1280]{0,1:T(8,128)S(1)}, f32[256,1280]{0,1:T(8,128)S(1)}, u32[]{:S(2)}, u32[]{:S(2)}) collective-permute-start(f32[256,1280]{0,1:T(8,128)S(1)} %get-tuple-element.397), channel_id=1, source_target_pairs={{0,1},{1,2},{2,3},{3,4},{4,5},{5,6},{6,7},{7,8},{8,9},{9,10},{10,1... | collective-permute-start | bytes 3932168 | tf_op jit(solution)/shard_map/ppermute | solution.py:16
  301.0 35.2 %collective-permute-start.11 = (f32[256,1280]{0,1:T(8,128)S(1)}, f32[256,1280]{0,1:T(8,128)S(1)}, u32[]{:S(2)}, u32[]{:S(2)}) collective-permute-start(f32[256,1280]{0,1:T(8,128)S(1)} %get-tuple-element.396), channel_id=1, source_target_pairs={{0,2},{1,3},{2,4},{3,5},{4,6},{5,7},{6,8},{7,9},{8,10},{9,11},{10,... | collective-permute-start | bytes 3932168 | tf_op jit(solution)/shard_map/ppermute | solution.py:16
  307.1 38.1 %collective-permute-start.8 = (f32[256,1280]{0,1:T(8,128)S(1)}, f32[256,1280]{0,1:T(8,128)S(1)}, u32[]{:S(2)}, u32[]{:S(2)}) collective-permute-start(f32[256,1280]{0,1:T(8,128)S(1)} %get-tuple-element.394), channel_id=1, source_target_pairs={{2,0},{3,1},{4,2},{5,3},{6,4},{7,5},{8,6},{9,7},{10,8},{11,9},{12,... | collective-permute-start | bytes 3932168 | tf_op jit(solution)/shard_map/ppermute | solution.py:16
  309.0 44.5 %copy-start.2 = (bf16[1,256,1280]{2,1,0:T(8,128)(2,1)S(1)}, bf16[1,256,1280]{2,1,0:T(8,128)(2,1)}, u32[]{:S(2)}) copy-start(bf16[1,256,1280]{2,1,0:T(8,128)(2,1)} %param.32) | copy-start | bytes 1966084
  309.0 44.5 %copy-start.9 = (bf16[10,256,64]{1,2,0:T(8,128)(2,1)S(1)}, bf16[10,256,64]{1,2,0:T(8,128)(2,1)}, u32[]{:S(2)}) copy-start(bf16[10,256,64]{1,2,0:T(8,128)(2,1)} %get-tuple-element.299) | copy-start | bytes 983044
  309.0 43.2 %collective-permute-start.9 = (f32[256,1280]{0,1:T(8,128)S(1)}, f32[256,1280]{0,1:T(8,128)S(1)}, u32[]{:S(2)}, u32[]{:S(2)}) collective-permute-start(f32[256,1280]{0,1:T(8,128)S(1)} %get-tuple-element.395), channel_id=1, source_target_pairs={{1,0},{2,1},{3,2},{4,3},{5,4},{6,5},{7,6},{8,7},{9,8},{10,9},{11,1... | collective-permute-start | bytes 3932168 | tf_op jit(solution)/shard_map/ppermute | solution.py:16
  352.6 0.8 copy-start.6
  358.8 127.8 %copy-start.13 = (u32[256]{0:T(256)S(1)}, u32[256]{0:T(256)}, u32[]{:S(2)}) copy-start(u32[256]{0:T(256)} %constant.302) | copy-start | bytes 3076
  358.8 284.7 %copy-start.3 = (bf16[1,256,1280]{2,1,0:T(8,128)(2,1)S(1)}, bf16[1,256,1280]{2,1,0:T(8,128)(2,1)}, u32[]{:S(2)}) copy-start(bf16[1,256,1280]{2,1,0:T(8,128)(2,1)} %param.32) | copy-start | bytes 1966084
  358.8 284.7 %copy-start.7 = (bf16[256,1280]{0,1:T(8,128)(2,1)S(1)}, bf16[256,1280]{0,1:T(8,128)(2,1)}, u32[]{:S(2)}) copy-start(bf16[256,1280]{0,1:T(8,128)(2,1)} %copy-done.6) | copy-start | bytes 1966084
  358.9 284.7 %copy-start.10 = (bf16[10,256,64]{1,2,0:T(8,128)(2,1)S(1)}, bf16[10,256,64]{1,2,0:T(8,128)(2,1)}, u32[]{:S(2)}) copy-start(bf16[10,256,64]{1,2,0:T(8,128)(2,1)} %get-tuple-element.299) | copy-start | bytes 983044
  358.9 436.7 %all-reduce.3.cloned.1.call-start = ((), (), s32[]{:S(2)}) async-start(), calls=%async_computation.8 | async-start | bytes 409600
  486.5 395.6 %reduce-scatter.11.cloned.1.call-start = ((), (), s32[]{:S(2)}) async-start(), calls=%async_computation.7 | async-start | bytes 696320
  643.6 4.2 copy-start.8
Sparse Core Ops, SparseCore 0:
  21.9 118.2 all-gather.1
  296.9 189.4 reduce-scatter.8
  491.3 150.0 reduce-scatter.6
  643.8 151.6 all-reduce.2
  797.9 84.2 reduce-scatter.10
